TPU v7x, 256 devices: a whole 4x4x8 slice. The times are simulated.
256 devices in a mesh: row: 8 (over y, core), col: 32 (over z, x).
Axes of the slice: x: 4, y: 4, z: 8, core: 2. Of those that a mesh axis runs over, the one named last changes fastest.
Arguments:
- hidden: bfloat16 [1024, 24576], P(None, 'row'), may hold values from -6 to 6
- down_weight: bfloat16 [24576, 6144], P('row', 'col'), may hold values from -0.0390625 to 0.0390625
- residual: bfloat16 [1024, 6144], P('row', 'col'), may hold values from -260 to 260
- gain: bfloat16 [6144], P('col'), may hold values from 0.099609375 to 1.8984375
- qk_weight: bfloat16 [6144, 12288], P(None, 'col'), may hold values from -0.078125 to 0.078125
Outputs:
- stream: bfloat16 [1024, 6144], P('row', 'col')
- queries_keys: bfloat16 [1024, 12288], P('row', 'col')
All inputs are finite; a program needn't handle non-finite values.
Results may differ from a plain program's by a relative error of at most 0.015.
Values may be sent and summed in bfloat16 or wider, within the bound.
A program may use at most 64 MiB of HBM per device.

v0:
```python
import jax
import jax.numpy as jnp
from jax import lax
from jax.sharding import PartitionSpec as P


def joined(value, axis, join):
    pieces = jax.tree.map(lambda part: lax.all_gather(part, axis), value)
    head = jax.tree.map(lambda part: part[0], pieces)
    tail = jax.tree.map(lambda part: part[1:], pieces)
    total, _ = lax.scan(lambda total, section: (join(total, section), None), head, tail)
    return total


def combine_moments(first, second):
    count_a, mean_a, spread_a = first
    count_b, mean_b, spread_b = second
    count = count_a + count_b
    delta = mean_b - mean_a
    mean = mean_a + delta * count_b / count
    spread = spread_a + spread_b + delta * delta * count_a * count_b / count
    return (count, mean, spread)


def per_device(hidden, down_weight, residual, gain, qk_weight):
    tok_rows = residual.shape[0]
    mlp = lax.psum_scatter(
        jnp.dot(hidden, down_weight, preferred_element_type=jnp.float32).astype(jnp.bfloat16),
        "row",
        scatter_dimension=0,
        tiled=True,
    ).astype(jnp.float32)
    stream = (residual.astype(jnp.float32) + mlp).astype(jnp.bfloat16)
    values = stream.astype(jnp.float32)
    local_width = values.shape[1]
    local_mean = jnp.mean(values, axis=1)
    local_dev = values - local_mean[:, None]
    local_spread = jnp.sum(local_dev * local_dev, axis=1)
    counts = jnp.full((tok_rows,), float(local_width), jnp.float32)
    total_count, mean_flat, spread_flat = joined(
        (counts, local_mean, local_spread), "col", combine_moments
    )
    mean = mean_flat[:, None]
    var = (spread_flat / total_count)[:, None]
    normed = ((values - mean) / jnp.sqrt(var + 1e-06) * gain.astype(jnp.float32)[None, :]).astype(
        jnp.bfloat16
    )
    product = jnp.dot(
        lax.all_gather(normed, "col", axis=1, tiled=True),
        qk_weight,
        preferred_element_type=jnp.float32,
    )
    return (stream, product.astype(jnp.bfloat16))


def solution(mesh):
    placed = (P(None, "row"), P("row", "col"), P("row", "col"), P("col"), P(None, "col"))
    return jax.shard_map(
        per_device,
        mesh=mesh,
        in_specs=placed,
        out_specs=(P("row", "col"), P("row", "col")),
        check_vma=False,
    )
```

profile of v0, /device:TPU:8, one launch (start us, length us, event | category | flops | bytes accessed | tf_op | source)
XLA Modules:
  0.0 214.9 jit_solution(6401340985521224175)
XLA Ops:
  7.2 0.0 copy-start
  7.2 0.0 copy-start.3
  7.2 0.0 copy-start.2
  7.2 0.0 reduce-scatter.4.cloned.1.call-start
  7.2 1.2 copy-done
  8.4 5.0 %convolution_convert_fusion = bf16[1024,192]{0,1:T(8,128)(2,1)S(1)} fusion(bf16[1024,3072]{1,0:T(8,128)(2,1)} %param.7, bf16[3072,192]{0,1:T(8,128)(2,1)S(1)} %copy-done), kind=kOutput, calls=%fused_computation.6 | convolution fusion | flops 1208156160 | bytes 7864320 | tf_op jit(solution)/shard_map/dot_general | solution.py:28
  13.4 1.0 copy.7
  14.4 0.0 reduce-scatter.4.cloned.1.call-update
  14.5 0.0 all-gather.6.cloned.1.call-start
  14.5 0.0 copy-done.3
  14.5 33.4 %reduce-scatter.4.cloned.1.call-done = bf16[128,192]{1,0:T(8,128)(2,1)} async-done(((bf16[1024,192]{1,0:T(8,128)(2,1)}), bf16[128,192]{1,0:T(8,128)(2,1)}) %reduce-scatter.4.cloned.1.call-update) | async-done | bytes 49168
  48.0 0.9 copy.8
  48.9 0.0 copy-done.2
  49.0 0.0 copy-start.1
  49.0 40.2 %all-gather.3 = f32[32,1,128]{2,1,0:T(1,128)S(1)} all-gather(f32[1,1,128]{2,1,0:T(1,128)S(1)} %bitcast.36), channel_id=3, replica_groups=mesh['row'=8,'col'=32] {'col'}, dimensions={0}, use_global_device_ids=true | all-gather | bytes 16896 | tf_op jit(solution)/shard_map/all_gather | solution.py:8
  89.3 36.5 %all-gather.2 = f32[32,1,128]{2,1,0:T(1,128)S(1)} all-gather(f32[1,1,128]{2,1,0:T(1,128)S(1)} %get-tuple-element.100), channel_id=2, replica_groups=mesh['row'=8,'col'=32] {'col'}, dimensions={0}, use_global_device_ids=true | all-gather | bytes 16896 | tf_op jit(solution)/shard_map/all_gather | solution.py:8
  125.8 2.0 while.16
  127.8 0.7 fusion.5
  128.5 0.0 all-gather.6.cloned.1.call-update
  128.5 75.0 %all-gather.6.cloned.1.call-done = bf16[128,6144]{0,1:T(8,128)(2,1)} async-done(((bf16[128,192]{0,1:T(8,128)(2,1)}), bf16[128,6144]{0,1:T(8,128)(2,1)}) %all-gather.6.cloned.1.call-update) | async-done | bytes 1572880 | tf_op jit(solution)/shard_map/all_gather | solution.py:49
  203.5 4.5 %convolution_convert_fusion.1 = bf16[128,384]{1,0:T(8,128)(2,1)} fusion(bf16[128,6144]{0,1:T(8,128)(2,1)} %all-gather.6.cloned.1.call-done, bf16[6144,384]{1,0:T(8,128)(2,1)} %param.11), kind=kOutput, calls=%fused_computation.7 | convolution fusion | flops 604028928 | bytes 6389760 | tf_op jit(solution)/shard_map/dot_general | solution.py:48
  208.0 0.0 copy-done.1
  (74 shorter events, 1.5 us)
Async XLA Ops:
  7.2 1.3 copy-start
  7.2 7.3 %copy-start.3 = (bf16[192]{0:T(256)(128)(2,1)S(1)}, bf16[192]{0:T(256)(128)(2,1)}, u32[]{:S(2)}) copy-start(bf16[192]{0:T(256)(128)(2,1)} %param.10) | copy-start | bytes 1156
  7.2 41.7 %copy-start.2 = (bf16[128,192]{0,1:T(8,128)(2,1)S(1)}, bf16[128,192]{0,1:T(8,128)(2,1)}, u32[]{:S(2)}) copy-start(bf16[128,192]{0,1:T(8,128)(2,1)} %param.9) | copy-start | bytes 147460
  7.2 40.8 %reduce-scatter.4.cloned.1.call-start = ((), (), s32[]{:S(2)}) async-start(), calls=%async_computation.2 | async-start | bytes 589824
  14.5 189.1 %all-gather.6.cloned.1.call-start = ((), (), s32[]{:S(2)}) async-start(), calls=%async_computation.1 | async-start | bytes 1622016 | tf_op jit(solution)/shard_map/all_gather | solution.py:49
  49.0 159.0 %copy-start.1 = (bf16[128,192]{0,1:T(8,128)(2,1)}, bf16[128,192]{0,1:T(8,128)(2,1)S(1)}, u32[]{:S(2)}) copy-start(bf16[128,192]{0,1:T(8,128)(2,1)S(1)} %get-tuple-element.98) | copy-start | bytes 147460
Sparse Core Ops, SparseCore 0:
  14.6 33.3 reduce-scatter.3
  128.6 74.8 all-gather.5
where the time goes:
time: 215 us
  waiting for transfers between devices  108 us (50%)
  blocking collectives  76.7 us (36%)
  between operations  14.1 us (7%)
  matrix products  9.48 us (4%)
  local copies, waits for them, and re-layouts  3.16 us (1%)
  other arithmetic  2.24 us (1%)
    all_gather x2, blocking collectives, joined(): pieces = jax.tree.map(lambda part: lax.all_gather(part, axis), value)  76.7 us
    all_gather x1, waiting for transfers between devices, per_device(): lax.all_gather(normed, 'col', axis=1, tiled=True)  75 us
    unnamed x3, waiting for transfers between devices  33.5 us
    dot_general x1, matrix products, per_device(): jnp.dot(hidden, down_weight, preferred_element_type=jnp.float32)  4.99 us
    dot_general x1, matrix products, per_device(): jnp.dot(lax.all_gather(normed, 'col', axis=1, tiled=True), qk_weight, pre...  4.49 us
  transfers between devices with their start and end apart: 2, of which 2 were waited for; matrix products, arithmetic and copies ran while one was open for 0% of the time, Pallas kernels for 0%

commit v1 on v0

--- a/solution.py
+++ b/solution.py
@@ -46,7 +46,9 @@
         jnp.bfloat16
     )
     product = jnp.dot(
-        lax.all_gather(normed, "col", axis=1, tiled=True),
+        jnp.concatenate(
+            lax.all_to_all(jnp.stack([normed] * lax.axis_size("col")), "col", 0, 0), axis=1
+        ),
         qk_weight,
         preferred_element_type=jnp.float32,
     )

time: 215 us -> 173 us (0.80)
  the two profiles are of different devices: /device:TPU:8 before, /device:TPU:2 now
where the time goes in v1:
time: 173 us
  blocking collectives  110 us (64%)
  waiting for transfers between devices  36.6 us (21%)
  between operations  14.2 us (8%)
  matrix products  6.65 us (4%)
  local copies, waits for them, and re-layouts  3.53 us (2%)
    all_gather x2, blocking collectives, joined(): pieces = jax.tree.map(lambda part: lax.all_gather(part, axis), value)  77.5 us
    unnamed x2, waiting for transfers between devices  36.6 us
    all_to_all x1, blocking collectives, per_device(): lax.all_to_all(jnp.stack([normed] * lax.axis_size('col')), 'col', 0, 0)  32.4 us
    dot_general x1, matrix products, per_device(): jnp.dot(hidden, down_weight, preferred_element_type=jnp.float32)  4.99 us
  transfers between devices with their start and end apart: 1, of which 1 were waited for; matrix products, arithmetic and copies ran while one was open for 0% of the time, Pallas kernels for 0%

profile of v1, /device:TPU:2, one launch (start us, length us, event | category | flops | bytes accessed | tf_op | source)
XLA Modules:
  0.0 173.0 jit_solution(764822216549478981)
XLA Ops:
  7.2 0.0 copy-start
  7.2 0.0 copy-start.4
  7.2 0.0 reduce-scatter.4.cloned.1.call-start
  7.2 1.2 copy-done
  8.4 5.0 %convolution_convert_fusion = bf16[1024,192]{0,1:T(8,128)(2,1)S(1)} fusion(bf16[1024,3072]{1,0:T(8,128)(2,1)} %param.7, bf16[3072,192]{0,1:T(8,128)(2,1)S(1)} %copy-done), kind=kOutput, calls=%fused_computation.6 | convolution fusion | flops 1208156160 | bytes 7864320 | tf_op jit(solution)/shard_map/dot_general | solution.py:28
  13.4 0.0 copy-start.3
  13.4 1.0 copy.8
  14.4 0.0 reduce-scatter.4.cloned.1.call-update
  14.5 0.0 copy-done.4
  14.5 36.6 %reduce-scatter.4.cloned.1.call-done = bf16[128,192]{1,0:T(8,128)(2,1)} async-done(((bf16[1024,192]{1,0:T(8,128)(2,1)}), bf16[128,192]{1,0:T(8,128)(2,1)}) %reduce-scatter.4.cloned.1.call-update) | async-done | bytes 49168
  51.1 0.9 copy.9
  52.0 0.0 copy-done.3
  52.1 0.0 copy-start.2
  52.1 39.9 %all-gather.3 = f32[32,1,128]{2,1,0:T(1,128)S(1)} all-gather(f32[1,1,128]{2,1,0:T(1,128)S(1)} %bitcast.40), channel_id=3, replica_groups=mesh['row'=8,'col'=32] {'col'}, dimensions={0}, use_global_device_ids=true | all-gather | bytes 16896 | tf_op jit(solution)/shard_map/all_gather | solution.py:8
  92.0 37.6 %all-gather.2 = f32[32,1,128]{2,1,0:T(1,128)S(1)} all-gather(f32[1,1,128]{2,1,0:T(1,128)S(1)} %get-tuple-element.100), channel_id=2, replica_groups=mesh['row'=8,'col'=32] {'col'}, dimensions={0}, use_global_device_ids=true | all-gather | bytes 16896 | tf_op jit(solution)/shard_map/all_gather | solution.py:8
  129.7 2.0 %while.16 = (s32[]{:T(128)}, f32[128]{0:T(128)S(1)}, f32[128]{0:T(128)S(1)}, f32[128]{0:T(128)S(1)}, f32[31,128]{1,0:T(8,128)S(1)}, /*index=5*/f32[31,128]{1,0:T(8,128)S(1)}, s32[]{:T(128)}, s32[]{:T(128)}) while((s32[]{:T(128)}, f32[128]{0:T(128)S(1)}, f32[128]{0:T(128)S(1)}, f32[128]{0:T(128)S(1)}, f32[31,128]{1,0:T(8,128)S(1)}, ...), condition=%wide.region_4.5_spmd.clone, body=%wide.region_3.4_spmd.clone.sunk | while | flops 1667 | bytes 5743 | solution.py:11
  131.7 0.1 fusion.5
  131.8 0.0 copy-start.1
  131.8 0.3 stack.2
  132.1 32.4 %all_to_all.5 = bf16[32,128,192]{1,2,0:T(8,128)(2,1)S(1)} all-to-all(bf16[32,128,192]{1,2,0:T(8,128)(2,1)S(1)} %stack.2), channel_id=1, replica_groups=mesh['row'=8,'col'=32] {'col'}, dimensions={0} | all-to-all | bytes 3145728 | tf_op jit(solution)/shard_map/all_to_all | solution.py:50
  164.5 0.0 copy-done.2
  164.5 0.0 copy-done.1
  164.5 1.7 convolution_convert_fusion.1
  (74 shorter events, 1.5 us)
Async XLA Ops:
  7.2 1.3 copy-start
  7.2 7.3 %copy-start.4 = (bf16[192]{0:T(256)(128)(2,1)S(1)}, bf16[192]{0:T(256)(128)(2,1)}, u32[]{:S(2)}) copy-start(bf16[192]{0:T(256)(128)(2,1)} %param.10) | copy-start | bytes 1156
  7.2 43.9 %reduce-scatter.4.cloned.1.call-start = ((), (), s32[]{:S(2)}) async-start(), calls=%async_computation.2 | async-start | bytes 589824
  13.4 38.6 %copy-start.3 = (bf16[128,192]{0,1:T(8,128)(2,1)S(1)}, bf16[128,192]{0,1:T(8,128)(2,1)}, u32[]{:S(2)}) copy-start(bf16[128,192]{0,1:T(8,128)(2,1)} %param.9) | copy-start | bytes 147460
  52.1 112.4 %copy-start.2 = (bf16[128,192]{0,1:T(8,128)(2,1)}, bf16[128,192]{0,1:T(8,128)(2,1)S(1)}, u32[]{:S(2)}) copy-start(bf16[128,192]{0,1:T(8,128)(2,1)S(1)} %get-tuple-element.98) | copy-start | bytes 147460
  131.8 32.7 %copy-start.1 = (bf16[6144,384]{1,0:T(8,128)(2,1)S(1)}, bf16[6144,384]{1,0:T(8,128)(2,1)}, u32[]{:S(2)}) copy-start(bf16[6144,384]{1,0:T(8,128)(2,1)} %param.11) | copy-start | bytes 14155780
Sparse Core Ops, SparseCore 0:
  14.6 36.4 reduce-scatter.3
